TPU v7x, 32 devices: a whole 2x2x4 slice. The times are simulated.
32 devices in a mesh: dp: 8 (over z, core), seq: 4 (over y, x).
Axes of the slice: x: 2, y: 2, z: 4, core: 2. Of those that a mesh axis runs over, the one named last changes fastest.
Arguments:
- tokens: int32 [8, 65536], P('dp', 'seq'), may hold values from 0 to 4
- stem_weight: bfloat16 [60, 768], replicated, may hold values from -1.5 to 1.5
- stem_bias: float32 [768], replicated, may hold values from -3 to 3
- conv_gain: float32 [768], replicated, may hold values from 0.1 to 1.9
- conv_weight: bfloat16 [5, 768, 1536], P(None, 'dp'), may hold values from -0.09375 to 0.09375
- conv_bias: float32 [1536], replicated, may hold values from -3 to 3
- attn_gain: float32 [1536], replicated, may hold values from 0.1 to 1.9
- w_query: bfloat16 [1536, 1024], P('dp'), may hold values from -7 to 7
- w_key: bfloat16 [1536, 128], P('dp'), may hold values from -0.15625 to 0.15625
- w_value: bfloat16 [1536, 192], P('dp'), may hold values from -0.15625 to 0.15625
- w_out: bfloat16 [1536, 1536], P('dp'), may hold values from -0.4375 to 0.4375
Outputs:
- features: bfloat16 [8, 512, 1536], P('dp', 'seq')
Inputs may be any that keep to these rules, and one draw needn't show every extreme that they name: `tokens`: 0 is an unknown base; 1 to 4 are A, C, G, T.
All inputs are finite; a program needn't handle non-finite values.
Results may differ from a plain program's by a relative error of at most 0.009.
The roundings to bfloat16 on the way count: a program that leaves them out, or rounds other values in their place, can miss the bound.
Values may be sent and summed in bfloat16 or wider, within the bound.
A program may use at most 192 MiB of HBM per device.

v0:
```python
import jax
import jax.numpy as jnp
from jax import lax
from jax.sharding import PartitionSpec as P

HEADS = 8
HEAD_K = 128
HEAD_V = 192
KW_STEM = 15
KW = 5
POOL_A = 8
POOL_B = 16


epsilon = 1e-06


def with_halo(block, sides, width):
    for axis, dim in sides:
        count = lax.axis_size(axis)
        forward = [(i, i + 1) for i in range(count - 1)]
        backward = [(target, source) for source, target in forward]
        low = lax.ppermute(
            lax.slice_in_dim(block, block.shape[dim] - width, None, axis=dim), axis, forward
        )
        high = lax.ppermute(lax.slice_in_dim(block, 0, width, axis=dim), axis, backward)
        block = jnp.concatenate([low, block, high], axis=dim)
    return block


def stem_pool(padded_tokens, count, stem_weight, stem_bias):
    columns = jnp.stack(
        [padded_tokens[offset : offset + count] for offset in range(KW_STEM)], axis=1
    )
    codes = jnp.arange(1, 5, dtype=jnp.int32)
    onehot = (columns[:, :, None] == codes).astype(jnp.bfloat16).reshape(count, KW_STEM * 4)
    block_len = min(count, 1024)
    onehot = onehot.reshape(count // block_len, block_len, KW_STEM * 4)

    def one_block(inputs):
        stem_rows = jnp.dot(inputs, stem_weight, preferred_element_type=jnp.float32) + stem_bias
        return jax.nn.gelu(jnp.max(stem_rows.reshape(block_len // POOL_A, POOL_A, -1), axis=1))

    return lax.map(one_block, onehot).reshape(count // POOL_A, -1).astype(jnp.bfloat16)


def rms_scale(values, gain):
    return values * lax.rsqrt(jnp.mean(values * values, axis=-1, keepdims=True) + epsilon) * gain


def rotate(values, angles):
    half_dim = values.shape[-1] // 2
    first = values[..., :half_dim]
    second = values[..., half_dim:]
    cosine = jnp.cos(angles)
    sine = jnp.sin(angles)
    return jnp.concatenate(
        [first * cosine - second * sine, second * cosine + first * sine], axis=-1
    )


def body(
    tokens,
    stem_weight,
    stem_bias,
    conv_gain,
    conv_weight,
    conv_bias,
    attn_gain,
    w_query,
    w_key,
    w_value,
    w_out,
):
    seq_local = tokens.shape[1]
    rows_enc = seq_local // POOL_A
    rows_att = rows_enc // POOL_B
    reach = KW_STEM // 2
    edge_rows = KW // 2
    extra_bases = edge_rows * POOL_A
    padded_tokens = with_halo(tokens, (("seq", 1),), reach + extra_bases)[0]
    left_pool = stem_pool(
        padded_tokens[: extra_bases + 2 * reach], extra_bases, stem_weight, stem_bias
    )
    middle_pool = stem_pool(
        padded_tokens[extra_bases : extra_bases + seq_local + 2 * reach],
        seq_local,
        stem_weight,
        stem_bias,
    )
    right_pool = stem_pool(
        padded_tokens[extra_bases + seq_local :], extra_bases, stem_weight, stem_bias
    )
    place = lax.axis_index("seq")
    last_place = lax.axis_size("seq") - 1
    left_norm = rms_scale(left_pool.astype(jnp.float32), conv_gain).astype(jnp.bfloat16)
    right_norm = rms_scale(right_pool.astype(jnp.float32), conv_gain).astype(jnp.bfloat16)
    left_norm = jnp.where(place > 0, left_norm, jnp.zeros_like(left_norm))
    right_norm = jnp.where(place < last_place, right_norm, jnp.zeros_like(right_norm))
    middle_norm = rms_scale(middle_pool.astype(jnp.float32), conv_gain).astype(jnp.bfloat16)
    padded_rows = jnp.concatenate([left_norm, middle_norm, right_norm], axis=0)
    out_channels = conv_weight.shape[2]
    full_weight = lax.all_gather(conv_weight, "dp", axis=1, tiled=True)
    conv_sum = jnp.dot(padded_rows[0:rows_enc], full_weight[0], preferred_element_type=jnp.float32)
    for tap_index in range(1, KW):
        conv_sum = conv_sum + jnp.dot(
            padded_rows[tap_index : tap_index + rows_enc],
            full_weight[tap_index],
            preferred_element_type=jnp.float32,
        )
    conv_sum = conv_sum + conv_bias
    coarse = jnp.max(jax.nn.gelu(conv_sum).reshape(rows_att, POOL_B, out_channels), axis=1).astype(
        jnp.bfloat16
    )
    residual = coarse.astype(jnp.float32)
    hidden = rms_scale(residual, attn_gain).astype(jnp.bfloat16)
    weight_rows = (
        lax.all_gather(w_query, "dp", axis=0, tiled=True),
        lax.all_gather(w_key, "dp", axis=0, tiled=True),
        lax.all_gather(w_value, "dp", axis=0, tiled=True),
    )
    inputs = hidden
    query, keys, values = tuple(
        (
            jnp.dot(inputs, rows_piece, preferred_element_type=jnp.float32)
            for rows_piece in weight_rows
        )
    )
    half_dim = HEAD_K // 2
    freqs = 10000.0 ** (-jnp.arange(half_dim, dtype=jnp.float32) / half_dim)
    positions = lax.axis_index("seq") * rows_att + jnp.arange(rows_att, dtype=jnp.int32)
    angles = positions.astype(jnp.float32)[:, None] * freqs[None, :]
    query = rotate(query.reshape(rows_att, HEADS, HEAD_K), angles[:, None, :]).astype(jnp.bfloat16)
    keys = rotate(keys, angles).astype(jnp.bfloat16)
    values = values.astype(jnp.bfloat16)
    keys_all, values_all = (
        lax.all_gather(keys, "seq", axis=0, tiled=True),
        lax.all_gather(values, "seq", axis=0, tiled=True),
    )
    scores = jnp.einsum(
        "rhd,kd->hrk", query, keys_all, preferred_element_type=jnp.float32
    ) * HEAD_K ** (-0.5)
    weights = jax.nn.softmax(scores, axis=-1).astype(jnp.bfloat16)
    mixed = jnp.einsum(
        "hrk,kd->rhd", weights, values_all, preferred_element_type=jnp.float32
    ).astype(jnp.bfloat16)
    mixed = mixed.reshape(rows_att, HEADS * HEAD_V)
    inputs = mixed
    projected = jnp.dot(
        inputs, lax.all_gather(w_out, "dp", axis=0, tiled=True), preferred_element_type=jnp.float32
    )
    return (residual + projected).astype(jnp.bfloat16)[None]


def solution(mesh):
    in_specs = (
        P("dp", "seq"),
        P(),
        P(),
        P(),
        P(None, "dp", None),
        P(),
        P(),
        P("dp", None),
        P("dp", None),
        P("dp", None),
        P("dp", None),
    )
    out_specs = P("dp", "seq", None)
    return jax.shard_map(body, mesh=mesh, in_specs=in_specs, out_specs=out_specs, check_vma=False)
```

profile of v0, /device:TPU:8, one launch (start us, length us, event | category | flops | bytes accessed | tf_op | source)
XLA Modules:
  0.0 250.1 jit_solution(2832627236857930586)
XLA Ops:
  8.8 3.4 %collective-permute-start = (s32[1,23]{1,0:T(1,128)S(1)}, s32[1,23]{1,0:T(1,128)S(1)}, u32[]{:S(2)}, u32[]{:S(2)}) collective-permute-start(s32[1,23]{1,0:T(1,128)S(1)} %get-tuple-element.116), channel_id=1, source_target_pairs={{0,1},{1,2},{2,3},{4,5},{5,6},{6,7},{8,9},{9,10},{10,11},{12,13},{... | collective-permute-start | bytes 284 | tf_op jit(solution)/shard_map/ppermute | solution.py:23
  13.7 20.2 %all_gather.22 = bf16[1536,192]{1,0:T(8,128)(2,1)} all-gather(bf16[192,192]{1,0:T(8,128)(2,1)} %param.22), channel_id=1, replica_groups=mesh['dp'=8,'seq'=4] {'dp'}, dimensions={0}, use_global_device_ids=true | all-gather | bytes 663552 | tf_op jit(solution)/shard_map/all_gather | solution.py:120
  33.9 19.0 %all_gather.24 = bf16[1536,128]{1,0:T(8,128)(2,1)} all-gather(bf16[192,128]{1,0:T(8,128)(2,1)S(1)} %copy-done.6), channel_id=1, replica_groups=mesh['dp'=8,'seq'=4] {'dp'}, dimensions={0}, use_global_device_ids=true | all-gather | bytes 442368 | tf_op jit(solution)/shard_map/all_gather | solution.py:119
  57.1 4.4 %stack.175 = s32[16384,15]{0,1:T(8,128)} concatenate(s32[16384,1]{0,1:T(1,128)} %get-tuple-element.110, s32[16384,1]{0,1:T(1,128)} %get-tuple-element.111, s32[16384,1]{0,1:T(1,128)} %get-tuple-element.112, s32[16384,1]{0,1:T(1,128)} %get-tuple-element.113, s32[16384,1]{0,1:T(1,128)} %get-tuple-element.114, s32[16384,1]{0,1:T(1,128)} %fusion.62, s32[16384,1]{0,1:T(1,128)} %get-tuple-element.109, ...), dimensions={1} | concatenate | bytes 1966080 | tf_op jit(solution)/shard_map/stack | solution.py:32
  61.5 4.1 %eq.66 = s32[16384,15,4]{0,2,1:T(4,128)} broadcast(s32[16384,15]{0,1:T(8,128)} %stack.175), dimensions={0,1} | broadcast | bytes 4915200 | tf_op jit(solution)/shard_map/eq | solution.py:36
  65.6 5.8 %eq.67 = s32[16,1024,60]{1,0,2:T(8,128)} reshape(s32[16384,15,4]{0,2,1:T(4,128)} %eq.66) | data formatting | bytes 7864320 | tf_op jit(solution)/shard_map/eq | solution.py:36
  71.4 3.8 %compare_convert_fusion = bf16[16,1024,60]{1,0,2:T(8,128)(2,1)} fusion(s32[16,1024,60]{1,0,2:T(8,128)} %eq.67, s32[60]{0:T(128)S(1)} %eq.63), kind=kLoop, calls=%fused_computation.27 | loop fusion | flops 1966080 | bytes 5898480 | tf_op jit(solution)/shard_map/convert_element_type | solution.py:36
  75.2 72.3 %while.2 = (s32[]{:T(128)}, bf16[16,128,768]{2,1,0:T(8,128)(2,1)S(1)}, bf16[16,1024,60]{1,0,2:T(8,128)(2,1)}, bf16[60,768]{1,0:T(8,128)(2,1)}, f32[768]{0:T(1024)S(1)}, /*index=5*/s32[]{:T(128)}) while((s32[]{:T(128)}, bf16[16,128,768]{2,1,0:T(8,128)(2,1)S(1)}, bf16[16,1024,60]{1,0,2:T(8,128)(2,1)}, bf16[60,768]{1,0:T(8,128)(2,1)}, ...), condition=%wide.region_4.5_spmd, body=%wide.region_2.4_spmd.sunk | while | flops 96632832 | bytes 1889357 | solution.py:44
  77.6 2.0 bitcast_reduce_fusion.4
  82.1 2.0 bitcast_reduce_fusion.4
  86.6 2.0 bitcast_reduce_fusion.4
  91.1 2.0 bitcast_reduce_fusion.4
  100.1 2.0 bitcast_reduce_fusion.4
  109.1 2.0 bitcast_reduce_fusion.4
  113.6 2.0 bitcast_reduce_fusion.4
  118.2 2.0 bitcast_reduce_fusion.4
  122.7 2.0 bitcast_reduce_fusion.4
  127.2 2.0 bitcast_reduce_fusion.4
  136.2 2.0 bitcast_reduce_fusion.4
  140.8 2.0 bitcast_reduce_fusion.4
  145.3 2.0 bitcast_reduce_fusion.4
  149.5 2.4 fusion.18
  151.9 2.4 multiply_convert_fusion
  154.4 10.7 %fusion.23 = f32[2048,1536]{1,0:T(8,128)} fusion(bf16[2,768]{1,0:T(2,128)(2,1)S(1)} %get-tuple-element.120, bf16[2048,768]{1,0:T(8,128)(2,1)} %fusion.18, bf16[5,768,1536]{2,1,0:T(8,128)(2,1)} %all-gather.4.cloned.1.call-done), kind=kOutput, calls=%fused_computation.35 | convolution fusion | flops 4838129664 | bytes 18091008 | tf_op jit(solution)/shard_map/dot_general | solution.py:104
  165.1 8.0 %fusion.26 = f32[2048,1536]{1,0:T(8,128)} fusion(bf16[2048,768]{1,0:T(8,128)(2,1)S(1)} %copy-done.1, bf16[2,768]{1,0:T(2,128)(2,1)S(1)} %get-tuple-element.120, bf16[5,768,1536]{2,1,0:T(8,128)(2,1)S(1)} %copy-done.10), kind=kOutput, calls=%fused_computation.39 | convolution fusion | flops 4838129664 | bytes 18091008 | tf_op jit(solution)/shard_map/dot_general | solution.py:106
  173.1 8.2 %fusion.20 = f32[2048,1536]{1,0:T(8,128)} fusion(bf16[2048,768]{1,0:T(8,128)(2,1)S(1)} %copy-done.1, bf16[2,768]{1,0:T(2,128)(2,1)S(1)} %get-tuple-element.121, bf16[5,768,1536]{2,1,0:T(8,128)(2,1)S(1)} %copy-done.10), kind=kOutput, calls=%fused_computation.33 | convolution fusion | flops 4838129664 | bytes 18091008 | tf_op jit(solution)/shard_map/dot_general | solution.py:106
  181.4 8.3 %fusion.29 = f32[2048,1536]{1,0:T(8,128)} fusion(bf16[2048,768]{1,0:T(8,128)(2,1)S(1)} %bitcast.187, bf16[5,768,1536]{2,1,0:T(8,128)(2,1)S(1)} %copy-done.10), kind=kOutput, calls=%fused_computation.46 | convolution fusion | flops 4831838208 | bytes 18087936 | tf_op jit(solution)/shard_map/dot_general | solution.py:106
  189.7 21.2 %bitcast_reduce_fusion.1 = bf16[128,1536]{1,0:T(8,128)(2,1)S(1)} fusion(f32[2048,1536]{1,0:T(8,128)} %fusion.20, f32[2048,1536]{1,0:T(8,128)} %fusion.29, f32[2048,1536]{1,0:T(8,128)} %fusion.23, f32[2048,1536]{1,0:T(8,128)} %fusion.26, f32[1536]{0:T(1024)S(1)} %copy-done.11, bf16[2,768]{1,0:T(2,128)(2,1)S(1)} %get-tuple-element.121, ...), kind=kOutput, calls=%fused_computation.21 | convolution fusion | flops 4881973248 | bytes 56239104 | tf_op jit(solution)/shard_map/dot_general | solution.py:106
  211.8 2.6 %convolution_bitcast_fusion = f32[16,8,8,128]{3,1,2,0:T(8,128)S(1)} fusion(bf16[1536,1024]{1,0:T(8,128)(2,1)} %all-gather.6.cloned.1.call-done, f32[1536]{0:T(1024)S(1)} %copy-done.8, f32[128]{0:T(128)S(1)} %add_rsqrt_fusion.1, bf16[128,1536]{1,0:T(8,128)(2,1)S(1)} %bitcast_reduce_fusion.1), kind=kOutput, calls=%fused_computation.57 | convolution fusion | flops 403439616 | bytes 4069888 | tf_op jit(solution)/shard_map/dot_general | solution.py:125
  214.5 15.0 %all_gather.25 = bf16[512,128]{0,1:T(8,128)(2,1)S(1)} all-gather(bf16[128,128]{0,1:T(8,128)(2,1)S(1)} %pad_maximum_fusion.4), channel_id=1, replica_groups=mesh['dp'=8,'seq'=4] {'seq'}, dimensions={0}, use_global_device_ids=true | all-gather | bytes 163840 | tf_op jit(solution)/shard_map/all_gather | solution.py:137
  229.9 7.4 %all_gather.23 = bf16[512,192]{0,1:T(8,128)(2,1)S(1)} all-gather(bf16[128,192]{0,1:T(8,128)(2,1)S(1)} %convolution_convert_fusion.1), channel_id=1, replica_groups=mesh['dp'=8,'seq'=4] {'seq'}, dimensions={0}, use_global_device_ids=true | all-gather | bytes 245760 | tf_op jit(solution)/shard_map/all_gather | solution.py:138
  239.7 3.9 %fusion.30 = bf16[1,128,1536]{2,1,0:T(8,128)(2,1)} fusion(bf16[128,1536]{0,1:T(8,128)(2,1)S(1)} %bitcast.189, bf16[1536,1536]{1,0:T(8,128)(2,1)} %all-gather.8.cloned.1.call-done, bf16[128,1536]{1,0:T(8,128)(2,1)S(1)} %bitcast_reduce_fusion.1), kind=kOutput, calls=%fused_computation.49 | convolution fusion | flops 604569600 | bytes 5898240 | tf_op jit(solution)/shard_map/dot_general | solution.py:149
  (130 shorter events, 59.8 us)
Async XLA Ops:
  6.5 46.4 %copy-start.3 = (s32[1,16384]{1,0:T(1,128)S(1)}, s32[1,16384]{1,0:T(1,128)}, u32[]{:S(2)}) copy-start(s32[1,16384]{1,0:T(1,128)} %param.13) | copy-start | bytes 196612
  6.5 27.4 %copy-start.6 = (bf16[192,128]{1,0:T(8,128)(2,1)S(1)}, bf16[192,128]{1,0:T(8,128)(2,1)}, u32[]{:S(2)}) copy-start(bf16[192,128]{1,0:T(8,128)(2,1)} %param.21) | copy-start | bytes 147460
  6.5 147.9 %all-gather.4.cloned.1.call-start = ((), (), s32[]{:S(2)}) async-start(), calls=%async_computation | async-start | bytes 13271040 | tf_op jit(solution)/shard_map/all_gather | solution.py:103
  7.3 204.6 %all-gather.6.cloned.1.call-start = ((), (), s32[]{:S(2)}) async-start(), calls=%async_computation.1 | async-start | bytes 3538944 | tf_op jit(solution)/shard_map/all_gather | solution.py:118
  8.0 231.7 %all-gather.8.cloned.1.call-start = ((), (), s32[]{:S(2)}) async-start(), calls=%async_computation.2 | async-start | bytes 5308416 | tf_op jit(solution)/shard_map/all_gather | solution.py:150
  8.8 44.1 %collective-permute-start = (s32[1,23]{1,0:T(1,128)S(1)}, s32[1,23]{1,0:T(1,128)S(1)}, u32[]{:S(2)}, u32[]{:S(2)}) collective-permute-start(s32[1,23]{1,0:T(1,128)S(1)} %get-tuple-element.116), channel_id=1, source_target_pairs={{0,1},{1,2},{2,3},{4,5},{5,6},{6,7},{8,9},{9,10},{10,11},{12,13},{... | collective-permute-start | bytes 284 | tf_op jit(solution)/shard_map/ppermute | solution.py:23
  12.2 42.3 %collective-permute-start.1 = (s32[1,23]{1,0:T(1,128)S(1)}, s32[1,23]{1,0:T(1,128)S(1)}, u32[]{:S(2)}, u32[]{:S(2)}) collective-permute-start(s32[1,23]{1,0:T(1,128)S(1)} %get-tuple-element.115), channel_id=1, source_target_pairs={{1,0},{2,1},{3,2},{5,4},{6,5},{7,6},{9,8},{10,9},{11,10},{13,12},{... | collective-permute-start | bytes 284 | tf_op jit(solution)/shard_map/ppermute | solution.py:26
  71.4 3.8 %copy-start.9 = (f32[768]{0:T(1024)S(1)}, f32[768]{0:T(1024)}, u32[]{:S(2)}) copy-start(f32[768]{0:T(1024)} %param.15) | copy-start | bytes 9220
  147.4 0.9 copy-start.5
  147.4 2.0 copy-start.7
  154.4 10.7 %copy-start.1 = (bf16[2048,768]{1,0:T(8,128)(2,1)S(1)}, bf16[2048,768]{1,0:T(8,128)(2,1)}, u32[]{:S(2)}) copy-start(bf16[2048,768]{1,0:T(8,128)(2,1)} %fusion.18) | copy-start | bytes 9437188
  154.4 10.7 %copy-start.10 = (bf16[5,768,1536]{2,1,0:T(8,128)(2,1)S(1)}, bf16[5,768,1536]{2,1,0:T(8,128)(2,1)}, u32[]{:S(2)}) copy-start(bf16[5,768,1536]{2,1,0:T(8,128)(2,1)} %all-gather.4.cloned.1.call-done) | copy-start | bytes 35389444
  173.1 8.2 %copy-start.2 = (bf16[16,128,768]{2,1,0:T(8,128)(2,1)S(1)}, bf16[16,128,768]{2,1,0:T(8,128)(2,1)}, u32[]{:S(2)}) copy-start(bf16[16,128,768]{2,1,0:T(8,128)(2,1)} %multiply_convert_fusion) | copy-start | bytes 9437188
  181.4 8.3 %copy-start.11 = (f32[1536]{0:T(1024)S(1)}, f32[1536]{0:T(1024)}, u32[]{:S(2)}) copy-start(f32[1536]{0:T(1024)} %param.18) | copy-start | bytes 18436
  189.6 21.4 %copy-start.4 = (bf16[1536,128]{1,0:T(8,128)(2,1)S(1)}, bf16[1536,128]{1,0:T(8,128)(2,1)}, u32[]{:S(2)}) copy-start(bf16[1536,128]{1,0:T(8,128)(2,1)} %all_gather.24) | copy-start | bytes 1179652
  189.6 21.4 %copy-start.8 = (f32[1536]{0:T(1024)S(1)}, f32[1536]{0:T(1024)}, u32[]{:S(2)}) copy-start(f32[1536]{0:T(1024)} %param.19) | copy-start | bytes 18436
  211.0 18.5 %copy-start = (bf16[1536,192]{1,0:T(8,128)(2,1)S(1)}, bf16[1536,192]{1,0:T(8,128)(2,1)}, u32[]{:S(2)}) copy-start(bf16[1536,192]{1,0:T(8,128)(2,1)} %all_gather.22) | copy-start | bytes 1769476
Sparse Core Ops, SparseCore 0:
  8.9 116.4 all-gather.3
  127.1 38.2 all-gather.5
  167.0 49.4 all-gather.7
where the time goes:
time: 253 us; the launch traced here: 250 us
  matrix products  97 us (38%)
  blocking collectives  61.6 us (24%)
  local copies, waits for them, and re-layouts  55.8 us (22%)
  other arithmetic  15.5 us (6%)
  between operations  13.4 us (5%)
  starting transfers between devices  4.75 us (2%)
    dot_general x4, matrix products, body(): jnp.dot(padded_rows[tap_index:tap_index + rows_enc], full_weight[tap_inde...  45.7 us
    dynamic_slice x32, local copies, waits for them, and re-layouts, stem_pool(): lax.map(one_block, onehot).reshape(count // POOL_A, -1).astype(jnp.bfloat16)  38.1 us
    dot_general x18, matrix products, one_block(): jnp.dot(inputs, stem_weight, preferred_element_type=jnp.float32) + stem_bias  32.1 us
    all_gather x1, blocking collectives, body(): lax.all_gather(w_value, 'dp', axis=0, tiled=True)  20.2 us
    all_gather x1, blocking collectives, body(): lax.all_gather(w_key, 'dp', axis=0, tiled=True)  19 us
    all_gather x1, blocking collectives, body(): lax.all_gather(keys, 'seq', axis=0, tiled=True)  15 us
    dot_general x1, matrix products, body(): jnp.dot(padded_rows[0:rows_enc], full_weight[0], preferred_element_type=j...  10.7 us
    eq x8, local copies, waits for them, and re-layouts, stem_pool(): columns[:, :, None] == codes  9.99 us
  transfers between devices with their start and end apart: 5, of which 0 were waited for; matrix products, arithmetic and copies ran while one was open for 66% of the time, Pallas kernels for 0%

commit v1 on v0

v1 whole, which is shorter than its diff:
```python
import functools

import jax
import jax.numpy as jnp
from jax import lax
from jax.experimental import pallas as pl
from jax.experimental.pallas import tpu as pltpu
from jax.sharding import PartitionSpec as P

HEADS = 8
HEAD_K = 128
HEAD_V = 192
KW_STEM = 15
KW = 5
POOL_A = 8
POOL_B = 16
GROUP = POOL_A * POOL_B
SPAN = 24

epsilon = 1e-06


def rms_scale(values, gain):
    return values * lax.rsqrt(jnp.mean(values * values, axis=-1, keepdims=True) + epsilon) * gain


def rotate(values, angles):
    half_dim = values.shape[-1] // 2
    first = values[..., :half_dim]
    second = values[..., half_dim:]
    cosine = jnp.cos(angles)
    sine = jnp.sin(angles)
    return jnp.concatenate(
        [first * cosine - second * sine, second * cosine + first * sine], axis=-1
    )


def stem_kernel(
    tok_ref, low_ref, high_ref, weight_ref, bias_ref, gain_ref, ext_ref, text_ref, hot_ref, shifted_ref, rows_ref
):
    count = tok_ref.shape[0]
    channels = weight_ref.shape[1]
    place = lax.axis_index("seq")
    last_place = lax.axis_size("seq") - 1
    main = tok_ref[...].astype(jnp.float32)
    row = lax.broadcasted_iota(jnp.int32, main.shape, 0)
    previous = jnp.where(row == 0, low_ref[...].astype(jnp.float32), pltpu.roll(main, 1, 0))
    following = jnp.where(
        row == count - 1, high_ref[...].astype(jnp.float32), pltpu.roll(main, count - 1, 0)
    )
    text_ref[0:SPAN, :] = previous.T[GROUP - SPAN :, :]
    text_ref[SPAN : SPAN + GROUP, :] = main.T
    text_ref[SPAN + GROUP :, :] = following.T[:SPAN, :]

    source = lax.broadcasted_iota(jnp.int32, (GROUP, weight_ref.shape[0]), 1)
    target = lax.broadcasted_iota(jnp.int32, (GROUP, weight_ref.shape[0]), 0)
    tap = source // 4
    base = source - 4 * tap
    for offset in range(POOL_A):
        pick = (target == base * SPAN + offset + tap + 1).astype(jnp.float32).astype(jnp.bfloat16)
        shifted_ref[offset] = jnp.dot(
            pick, weight_ref[...], preferred_element_type=jnp.float32
        ).astype(jnp.bfloat16)

    def hot_of(span):
        planes = [(span == float(code)).astype(jnp.float32) for code in range(1, 5)]
        planes.append(jnp.zeros((GROUP - 4 * SPAN, span.shape[1]), jnp.float32))
        return jnp.concatenate(planes, axis=0).T.astype(jnp.bfloat16)

    for j in range(POOL_B):
        hot_ref[j] = hot_of(text_ref[8 * j + SPAN - 8 : 8 * j + 2 * SPAN - 8, :])
    lane = lax.broadcasted_iota(jnp.int32, (SPAN, count), 1)
    edge = jnp.where(
        lane == 0,
        text_ref[0:SPAN, :],
        jnp.where(
            lane == 1,
            pltpu.roll(text_ref[8 : 8 + SPAN, :], 1, 1),
            jnp.where(
                lane == 2,
                pltpu.roll(text_ref[GROUP + SPAN - 8 : GROUP + 2 * SPAN - 8, :], 3, 1),
                pltpu.roll(text_ref[GROUP + SPAN : GROUP + 2 * SPAN, :], 4, 1),
            ),
        ),
    )
    hot_ref[POOL_B] = hot_of(edge)

    width = 256

    def block(j, carry):
        hot = hot_ref[j]
        for chunk in range(channels // width):
            columns = slice(chunk * width, (chunk + 1) * width)
            best = None
            for offset in range(POOL_A):
                stem = jnp.dot(
                    hot, shifted_ref[offset, :, columns], preferred_element_type=jnp.float32
                )
                best = stem if best is None else jnp.maximum(best, stem)
            pooled = jax.nn.gelu(best + bias_ref[:, columns]).astype(jnp.bfloat16)
            rows_ref[:, columns] = pooled.astype(jnp.float32)
        pooled = rows_ref[...]
        start = pl.multiple_of((j + 2) * count, count)
        ext_ref[pl.ds(start, count), :] = rms_scale(pooled, gain_ref[...]).astype(jnp.bfloat16)
        return carry

    lax.fori_loop(0, POOL_B + 1, block, 0)
    edges = ext_ref[(POOL_B + 2) * count : (POOL_B + 3) * count, :].astype(jnp.float32)
    left_keep = (place > 0).astype(jnp.float32)
    right_keep = (place < last_place).astype(jnp.float32)
    spot = lax.broadcasted_iota(jnp.int32, (count, channels), 0)
    for index in range(2):
        inner = ext_ref[(POOL_B + index) * count : (POOL_B + index + 1) * count, :]
        moved = pltpu.roll(inner.astype(jnp.float32), 1, 0)
        ext_ref[index * count : (index + 1) * count, :] = jnp.where(
            spot == 0, edges[index : index + 1, :] * left_keep, moved
        ).astype(jnp.bfloat16)
        inner = ext_ref[(2 + index) * count : (3 + index) * count, :]
        moved = pltpu.roll(inner.astype(jnp.float32), count - 1, 0)
        at = POOL_B + 2 + index
        ext_ref[at * count : (at + 1) * count, :] = jnp.where(
            spot == count - 1, edges[2 + index : 3 + index, :] * right_keep, moved
        ).astype(jnp.bfloat16)


def stem_stage(tokens, low, high, stem_weight, stem_bias, conv_gain):
    count = tokens.shape[0]
    channels = stem_weight.shape[1]
    return pl.pallas_call(
        stem_kernel,
        out_shape=jax.ShapeDtypeStruct(((POOL_B + 4) * count, channels), jnp.bfloat16),
        in_specs=[pl.BlockSpec(memory_space=pltpu.VMEM)] * 6,
        out_specs=pl.BlockSpec(memory_space=pltpu.VMEM),
        scratch_shapes=[
            pltpu.VMEM((GROUP + 2 * SPAN, count), jnp.float32),
            pltpu.VMEM((POOL_B + 1, count, GROUP), jnp.bfloat16),
            pltpu.VMEM((POOL_A, GROUP, channels), jnp.bfloat16),
            pltpu.VMEM((count, channels), jnp.float32),
        ],
        cost_estimate=pl.CostEstimate(
            flops=20_000_000_000, bytes_accessed=4_000_000, transcendentals=1_600_000
        ),
        name="stem_stage",
    )(tokens, low, high, stem_weight, stem_bias[None], conv_gain[None])


def conv_kernel(count, ext_ref, weight_ref, bias_ref, coarse_ref):
    group = 4
    width = weight_ref.shape[-1]
    channels = ext_ref.shape[1]

    def block(m, carry):
        most, least = carry
        total = None
        for tap in range(KW):
            start = pl.multiple_of((m * group + tap) * count, count)
            part = jnp.dot(
                ext_ref[pl.ds(start, group * count), :],
                weight_ref[:, :, 0, tap].reshape(channels, width),
                preferred_element_type=jnp.float32,
            )
            total = part if total is None else total + part
        for index in range(group):
            piece = total[index * count : (index + 1) * count]
            most = jnp.maximum(most, piece)
            least = jnp.minimum(least, piece)
        return most, least

    big = jnp.full((count, width), jnp.finfo(jnp.float32).max, jnp.float32)
    most, least = lax.fori_loop(0, POOL_B // group, block, (-big, big))
    bias = bias_ref[...]
    coarse_ref[...] = jnp.maximum(jax.nn.gelu(most + bias), jax.nn.gelu(least + bias)).astype(
        jnp.bfloat16
    )


def conv_stage(ext, weight, conv_bias):
    count = ext.shape[0] // (POOL_B + 4)
    ways, row_parts, column_parts, taps, depth, columns = weight.shape
    width = 256
    steps = columns // width
    return pl.pallas_call(
        functools.partial(conv_kernel, count),
        grid=(column_parts, steps),
        out_shape=jax.ShapeDtypeStruct((count, column_parts * columns), jnp.bfloat16),
        in_specs=[
            pl.BlockSpec(ext.shape, lambda b, n: (0, 0), pipeline_mode=pl.Buffered(1)),
            pl.BlockSpec(
                (ways, row_parts, 1, taps, depth, width), lambda b, n: (0, 0, b, 0, 0, n)
            ),
            pl.BlockSpec((1, width), lambda b, n: (0, b * steps + n)),
        ],
        out_specs=pl.BlockSpec((count, width), lambda b, n: (0, b * steps + n)),
        cost_estimate=pl.CostEstimate(
            flops=24_000_000_000, bytes_accessed=16_000_000, transcendentals=400_000
        ),
        name="conv_stage",
    )(ext, weight, conv_bias[None])


def gather_conv(conv_weight):
    taps, depth, columns = conv_weight.shape
    members = lax.axis_size("seq")
    place = lax.axis_index("seq")
    for row_parts in (2, 1, 3):
        column_parts = members // row_parts
        if members % row_parts or depth % (16 * row_parts) or columns % (256 * column_parts):
            continue
        depth_part = depth // row_parts
        column_part = columns // column_parts
        piece = lax.dynamic_slice(
            conv_weight,
            (0, place // column_parts * depth_part, place % column_parts * column_part),
            (taps, depth_part, column_part),
        )
        full = lax.all_gather(piece, ("dp", "seq"), axis=0, tiled=False)
        return full.reshape(-1, row_parts, column_parts, taps, depth_part, column_part)
    full = lax.all_gather(conv_weight, "dp", axis=0, tiled=False)
    return full[:, None, None]


def gather_rows(weight):
    members = lax.axis_size("seq")
    rows = weight.shape[0] // members
    piece = lax.dynamic_slice_in_dim(weight, lax.axis_index("seq") * rows, rows, axis=0)
    return lax.all_gather(piece, ("dp", "seq"), axis=0, tiled=True)


def body(
    tokens,
    stem_weight,
    stem_bias,
    conv_gain,
    conv_weight,
    conv_bias,
    attn_gain,
    w_query,
    w_key,
    w_value,
    w_out,
):
    seq_local = tokens.shape[1]
    rows_att = seq_local // GROUP
    full_conv = gather_conv(conv_weight)
    projections = gather_rows(jnp.concatenate([w_query, w_key, w_value], axis=1))
    full_out = gather_rows(w_out)
    tokens = tokens.reshape(rows_att, GROUP)
    size = lax.axis_size("seq")
    forward = [(i, i + 1) for i in range(size - 1)]
    backward = [(i + 1, i) for i in range(size - 1)]
    low = lax.ppermute(tokens[-1:], "seq", forward)
    high = lax.ppermute(tokens[:1], "seq", backward)
    ext = stem_stage(tokens, low, high, stem_weight, stem_bias, conv_gain)
    coarse = conv_stage(ext, full_conv, conv_bias)
    residual = coarse.astype(jnp.float32)
    hidden = rms_scale(residual, attn_gain).astype(jnp.bfloat16)
    projected = jnp.dot(hidden, projections, preferred_element_type=jnp.float32)
    split = HEADS * HEAD_K
    query = projected[:, :split]
    keys = projected[:, split : split + HEAD_K]
    values = projected[:, split + HEAD_K :]
    half_dim = HEAD_K // 2
    freqs = 10000.0 ** (-jnp.arange(half_dim, dtype=jnp.float32) / half_dim)
    positions = lax.axis_index("seq") * rows_att + jnp.arange(rows_att, dtype=jnp.int32)
    angles = positions.astype(jnp.float32)[:, None] * freqs[None, :]
    query = rotate(query.reshape(rows_att, HEADS, HEAD_K), angles[:, None, :]).astype(jnp.bfloat16)
    keys = rotate(keys, angles).astype(jnp.bfloat16)
    pair = jnp.concatenate([keys, values.astype(jnp.bfloat16)], axis=1)
    pair = lax.all_gather(pair, "seq", axis=0, tiled=True)
    keys_all, values_all = pair[:, :HEAD_K], pair[:, HEAD_K:]
    scores = jnp.einsum(
        "rhd,kd->hrk", query, keys_all, preferred_element_type=jnp.float32
    ) * HEAD_K ** (-0.5)
    weights = jax.nn.softmax(scores, axis=-1).astype(jnp.bfloat16)
    mixed = jnp.einsum(
        "hrk,kd->rhd", weights, values_all, preferred_element_type=jnp.float32
    ).astype(jnp.bfloat16)
    mixed = mixed.reshape(rows_att, HEADS * HEAD_V)
    out = jnp.dot(mixed, full_out, preferred_element_type=jnp.float32)
    return (residual + out).astype(jnp.bfloat16)[None]


def solution(mesh):
    in_specs = (
        P("dp", "seq"),
        P(),
        P(),
        P(),
        P(None, "dp", None),
        P(),
        P(),
        P("dp", None),
        P("dp", None),
        P("dp", None),
        P("dp", None),
    )
    out_specs = P("dp", "seq", None)
    return jax.shard_map(body, mesh=mesh, in_specs=in_specs, out_specs=out_specs, check_vma=False)
```

time: 253 us -> 244 us (0.964)
  waiting for transfers between devices: 1.49 us -> 142 us
  matrix products: 97 us -> 11.7 us
  blocking collectives: 61.6 us -> 9.79 us
  Pallas kernels: 0 us -> 48.6 us
  local copies, waits for them, and re-layouts: 55.8 us -> 8.71 us
  other arithmetic: 15.5 us -> 3.72 us
    all_gather x3, waiting for transfers between devices: 0.06 us -> 139 us  [the longest x2 74.1 us: gather_rows(): return lax.all_gather(piece, ('dp', 'seq'), axis=0, tiled=True)]
    dot_general x27 -> x2, matrix products: 95.7 us -> 8.06 us  [the longest x1 4.16 us: body(): projected = jnp.dot(hidden, projections, preferred_element_type=jnp.float32)]
    all_gather x4 -> x1, blocking collectives: 61.6 us -> 9.79 us  [body(): pair = lax.all_gather(pair, 'seq', axis=0, tiled=True)]
    pallas_call x0 -> x2, Pallas kernels: none -> 48.6 us  [the longest x1 33 us: conv_stage(): pl.pallas_call(functools.partial(conv_kernel, count), grid=(column_parts,...]
    dynamic_slice x32 -> x2, local copies, waits for them, and re-layouts: 38.1 us -> 2.35 us  [the longest x1 1.59 us: gather_rows(): lax.dynamic_slice_in_dim(weight, lax.axis_index('seq') * rows, rows, axis=0)]
    eq x8 -> x0, local copies, waits for them, and re-layouts: 9.99 us -> none  [stem_pool(): columns[:, :, None] == codes]
    convert_element_type x3 -> x0, other arithmetic: 8.66 us -> none  [the longest x2 4.85 us: body(): rms_scale(middle_pool.astype(jnp.float32), conv_gain).astype(jnp.bfloat16)]
    another operation x6 -> x0, local copies, waits for them, and re-layouts: 6.39 us -> none  [stem_pool(): jnp.stack([padded_tokens[offset:offset + count] for offset in range(KW_ST...]
  transfers between devices with their start and end apart: 5 -> 5, of which waited for: 0 -> 4; matrix products, arithmetic and copies ran while one was open for 66% -> 7% of each run, Pallas kernels for 0% -> 20%
where the time goes in v1:
time: 244 us; the launch traced here: 242 us
  waiting for transfers between devices  142 us (58%)
  Pallas kernels  48.6 us (20%)
  between operations  13.3 us (5%)
  matrix products  11.7 us (5%)
  blocking collectives  9.79 us (4%)
  local copies, waits for them, and re-layouts  8.71 us (4%)
  starting transfers between devices  4.79 us (2%)
  other arithmetic  3.72 us (2%)
    all_gather x2, waiting for transfers between devices, gather_rows(): return lax.all_gather(piece, ('dp', 'seq'), axis=0, tiled=True)  74.1 us
    all_gather x1, waiting for transfers between devices, gather_conv(): full = lax.all_gather(piece, ('dp', 'seq'), axis=0, tiled=False)  65.3 us
    pallas_call x1, Pallas kernels, conv_stage(): pl.pallas_call(functools.partial(conv_kernel, count), grid=(column_parts,...  33 us
    pallas_call x1, Pallas kernels, stem_stage(): pl.pallas_call(stem_kernel, out_shape=jax.ShapeDtypeStruct(((POOL_B + 4)...  15.6 us
    all_gather x1, blocking collectives, body(): pair = lax.all_gather(pair, 'seq', axis=0, tiled=True)  9.79 us
  transfers between devices with their start and end apart: 5, of which 4 were waited for; matrix products, arithmetic and copies ran while one was open for 7% of the time, Pallas kernels for 20%

profile of v1, /device:TPU:8, one launch (start us, length us, event | category | flops | bytes accessed | tf_op | source)
XLA Modules:
  0.0 242.4 jit_solution(17983693007419785133)
XLA Ops:
  6.6 1.3 copy-done
  7.9 0.8 constant_dynamic-slice_fusion.1
  8.7 0.0 all-gather.5.cloned.1.call-start
  8.7 1.6 fusion.21
  10.4 1.6 constant_dynamic-slice_fusion
  12.0 0.7 fusion.32
  12.7 3.4 %collective-permute-start = (s32[1,128]{1,0:T(1,128)S(1)}, s32[1,128]{1,0:T(1,128)S(1)}, u32[]{:S(2)}, u32[]{:S(2)}) collective-permute-start(s32[1,128]{1,0:T(1,128)S(1)} %get-tuple-element.12), channel_id=1, source_target_pairs={{0,1},{1,2},{2,3},{4,5},{5,6},{6,7},{8,9},{9,10},{10,11},{12,13},{... | collective-permute-start | bytes 1544 | tf_op jit(solution)/shard_map/ppermute | solution.py:251
  16.1 1.3 collective-permute-start.1
  17.4 0.6 broadcast_in_dim.8.bias_ref
  18.0 0.6 broadcast_in_dim.9.gain_ref
  18.6 0.6 broadcast_in_dim.10.bias_ref
  19.2 2.3 collective-permute-done.1.high_ref
  21.6 0.6 copy-done.8
  22.1 15.6 %stem_stage.1.ext_ref = bf16[2560,768]{1,0:T(8,128)(2,1)} custom-call(s32[128,128]{1,0:T(8,128)} %bitcast.38, s32[1,128]{1,0:T(1,128)} %copy-done.7, s32[1,128]{1,0:T(1,128)} %copy-done.8, bf16[60,768]{1,0:T(8,128)(2,1)} %weight_ref.1, f32[1,768]{1,0:T(1,128)} %broadcast_in_dim.8.bias_ref, f32[1,768]{1,0:T(1,128)} %broadcast_in_dim.9.gain_ref), custom_call_target="tpu_custom_call" | custom-call | flops 20000000000 | bytes 4000000 | tf_op jit(solution)/shard_map/stem_stage/pallas_call | solution.py:129
  37.7 65.3 %all-gather.9.cloned.1.call-done = bf16[160,48,768]{2,1,0:T(8,128)(2,1)} async-done(((bf16[5,48,768]{2,1,0:T(8,128)(2,1)}), bf16[160,48,768]{2,1,0:T(8,128)(2,1)}) %all-gather.9.cloned.1.call-update) | async-done | bytes 11796496 | tf_op jit(solution)/shard_map/all_gather | solution.py:216
  103.1 33.0 %conv_stage.1 = bf16[128,1536]{1,0:T(8,128)(2,1)} custom-call(bf16[2560,768]{1,0:T(8,128)(2,1)} %stem_stage.1.ext_ref, bf16[8,2,2,5,48,768]{5,4,3,2,1,0:T(8,128)(2,1)} %bitcast.39, f32[1,1536]{1,0:T(1,128)} %broadcast_in_dim.10.bias_ref), custom_call_target="tpu_custom_call" | custom-call | flops 24000000000 | bytes 16000000 | tf_op jit(solution)/shard_map/conv_stage/pallas_call | solution.py:182
  136.1 1.2 fusion.9
  137.2 29.6 %all-gather.5.cloned.1.call-done = bf16[1536,1344]{1,0:T(8,128)(2,1)} async-done(((bf16[48,1344]{1,0:T(8,128)(2,1)}), bf16[1536,1344]{1,0:T(8,128)(2,1)}) %all-gather.5.cloned.1.call-update) | async-done | bytes 4128784 | tf_op jit(solution)/shard_map/all_gather | solution.py:226
  166.8 4.2 %fusion.12 = f32[128,1344]{0,1:T(8,128)S(1)} fusion(bf16[1536,1344]{1,0:T(8,128)(2,1)} %all-gather.5.cloned.1.call-done, bf16[128,1536]{1,0:T(8,128)(2,1)} %conv_stage.1, f32[1536]{0:T(1024)S(1)} %copy-done.3, f32[128]{0:T(128)S(1)} %add_rsqrt_fusion), kind=kOutput, calls=%fused_computation.22 | convolution fusion | flops 529268736 | bytes 5216768 | tf_op jit(solution)/shard_map/dot_general | solution.py:257
  171.1 0.2 copy.27
  171.3 0.2 copy.28
  171.5 0.2 subtract_convert_fusion.1
  171.7 0.1 copy.19
  171.8 0.1 copy.21
  171.9 9.8 %all_gather.18 = bf16[512,320]{0,1:T(8,128)(2,1)S(1)} all-gather(bf16[128,320]{0,1:T(8,128)(2,1)S(1)} %pad_maximum_fusion), channel_id=1, replica_groups=mesh['dp'=8,'seq'=4] {'seq'}, dimensions={0}, use_global_device_ids=true | all-gather | bytes 409600 | tf_op jit(solution)/shard_map/all_gather | solution.py:269
  181.7 0.2 subtract_convert_fusion
  181.8 0.5 fusion.16
  182.4 1.3 copy-done.2
  183.7 0.6 fusion.33
  184.3 3.1 %convolution_convert_fusion = bf16[192,8,128]{2,0,1:T(8,128)(2,1)S(1)} fusion(f32[8,128]{1,0:T(8,128)S(1)} %fusion.33, bf16[512,320]{0,1:T(8,128)(2,1)S(1)} %all_gather.18, f32[512,128,8]{1,0,2:T(8,128)} %copy-done.2), kind=kOutput, calls=%fused_computation.10 | convolution fusion | flops 204146176 | bytes 4788224 | tf_op jit(solution)/shard_map/hrk,kd->rhd/dot_general | solution.py:275
  187.4 44.5 %all-gather.7.cloned.1.call-done = bf16[1536,1536]{1,0:T(8,128)(2,1)} async-done(((bf16[48,1536]{1,0:T(8,128)(2,1)}), bf16[1536,1536]{1,0:T(8,128)(2,1)}) %all-gather.7.cloned.1.call-update) | async-done | bytes 4718608 | tf_op jit(solution)/shard_map/all_gather | solution.py:226
  231.9 3.9 %fusion.2 = bf16[1,128,1536]{2,1,0:T(8,128)(2,1)} fusion(bf16[128,1536]{0,1:T(8,128)(2,1)S(1)} %bitcast.37, bf16[1536,1536]{1,0:T(8,128)(2,1)} %all-gather.7.cloned.1.call-done, bf16[128,1536]{1,0:T(8,128)(2,1)S(1)} %copy-done.1), kind=kOutput, calls=%fused_computation.3 | convolution fusion | flops 604569600 | bytes 5898240 | tf_op jit(solution)/shard_map/dot_general | solution.py:279
  (28 shorter events, 0.3 us)
Async XLA Ops:
  6.5 1.4 copy-start
  6.5 10.9 %copy-start.5 = (f32[768]{0:T(1024)S(1)}, f32[768]{0:T(1024)}, u32[]{:S(2)}) copy-start(f32[768]{0:T(1024)} %param.13) | copy-start | bytes 9220
  6.5 11.5 %copy-start.6 = (f32[768]{0:T(1024)S(1)}, f32[768]{0:T(1024)}, u32[]{:S(2)}) copy-start(f32[768]{0:T(1024)} %param.14) | copy-start | bytes 9220
  6.5 12.1 %copy-start.4 = (f32[1536]{0:T(1024)S(1)}, f32[1536]{0:T(1024)}, u32[]{:S(2)}) copy-start(f32[1536]{0:T(1024)} %param.16) | copy-start | bytes 18436
  6.5 96.5 %all-gather.9.cloned.1.call-start = ((), (), s32[]{:S(2)}) async-start(), calls=%async_computation.2 | async-start | bytes 12165120 | tf_op jit(solution)/shard_map/all_gather | solution.py:216
  8.7 158.1 %all-gather.5.cloned.1.call-start = ((), (), s32[]{:S(2)}) async-start(), calls=%async_computation | async-start | bytes 4460544 | tf_op jit(solution)/shard_map/all_gather | solution.py:226
  10.4 221.6 %all-gather.7.cloned.1.call-start = ((), (), s32[]{:S(2)}) async-start(), calls=%async_computation.1 | async-start | bytes 4866048 | tf_op jit(solution)/shard_map/all_gather | solution.py:226
  12.7 6.5 %collective-permute-start = (s32[1,128]{1,0:T(1,128)S(1)}, s32[1,128]{1,0:T(1,128)S(1)}, u32[]{:S(2)}, u32[]{:S(2)}) collective-permute-start(s32[1,128]{1,0:T(1,128)S(1)} %get-tuple-element.12), channel_id=1, source_target_pairs={{0,1},{1,2},{2,3},{4,5},{5,6},{6,7},{8,9},{9,10},{10,11},{12,13},{... | collective-permute-start | bytes 1544 | tf_op jit(solution)/shard_map/ppermute | solution.py:251
  16.1 5.5 %collective-permute-start.1 = (s32[1,128]{1,0:T(1,128)S(1)}, s32[1,128]{1,0:T(1,128)S(1)}, u32[]{:S(2)}, u32[]{:S(2)}) collective-permute-start(s32[1,128]{1,0:T(1,128)S(1)} %get-tuple-element.11), channel_id=1, source_target_pairs={{1,0},{2,1},{3,2},{5,4},{6,5},{7,6},{9,8},{10,9},{11,10},{13,12},{... | collective-permute-start | bytes 1544 | tf_op jit(solution)/shard_map/ppermute | solution.py:252
  19.2 2.3 copy-start.7
  21.6 0.6 copy-start.8
  103.1 63.7 %copy-start.3 = (f32[1536]{0:T(1024)S(1)}, f32[1536]{0:T(1024)}, u32[]{:S(2)}) copy-start(f32[1536]{0:T(1024)} %param.17) | copy-start | bytes 18436
  182.4 1.3 copy-start.2
  184.3 47.6 %copy-start.1 = (bf16[128,1536]{1,0:T(8,128)(2,1)S(1)}, bf16[128,1536]{1,0:T(8,128)(2,1)}, u32[]{:S(2)}) copy-start(bf16[128,1536]{1,0:T(8,128)(2,1)} %conv_stage.1) | copy-start | bytes 1179652
Sparse Core Ops, SparseCore 0:
  10.2 92.7 all-gather.8
  105.9 60.7 all-gather.4
  169.7 62.1 all-gather.6

commit v2 on v1

--- a/solution.py
+++ b/solution.py
@@ -38,15 +38,33 @@
 def stem_kernel(
     tok_ref, low_ref, high_ref, weight_ref, bias_ref, gain_ref, ext_ref, text_ref, hot_ref, shifted_ref, rows_ref
 ):
+    stem_compute(
+        tok_ref,
+        low_ref[...],
+        high_ref[...],
+        weight_ref,
+        bias_ref,
+        gain_ref,
+        ext_ref,
+        text_ref,
+        hot_ref,
+        shifted_ref,
+        rows_ref,
+    )
+
+
+def stem_compute(
+    tok_ref, low, high, weight_ref, bias_ref, gain_ref, ext_ref, text_ref, hot_ref, shifted_ref, rows_ref
+):
     count = tok_ref.shape[0]
     channels = weight_ref.shape[1]
     place = lax.axis_index("seq")
     last_place = lax.axis_size("seq") - 1
     main = tok_ref[...].astype(jnp.float32)
     row = lax.broadcasted_iota(jnp.int32, main.shape, 0)
-    previous = jnp.where(row == 0, low_ref[...].astype(jnp.float32), pltpu.roll(main, 1, 0))
+    previous = jnp.where(row == 0, low.astype(jnp.float32), pltpu.roll(main, 1, 0))
     following = jnp.where(
-        row == count - 1, high_ref[...].astype(jnp.float32), pltpu.roll(main, count - 1, 0)
+        row == count - 1, high.astype(jnp.float32), pltpu.roll(main, count - 1, 0)
     )
     text_ref[0:SPAN, :] = previous.T[GROUP - SPAN :, :]
     text_ref[SPAN : SPAN + GROUP, :] = main.T
@@ -198,6 +216,276 @@
     )(ext, weight, conv_bias[None])
 
 
+MESH = pl.DeviceIdType.MESH
+
+
+def encoder_kernel(
+    tok_ref,
+    stem_weight_ref,
+    stem_bias_ref,
+    gain_ref,
+    conv_bias_ref,
+    conv_ref,
+    attn_ref,
+    coarse_ref,
+    full_attn_ref,
+    text_ref,
+    hot_ref,
+    shifted_ref,
+    rows_ref,
+    ext_ref,
+    low_ref,
+    high_ref,
+    conv_full,
+    attn_full,
+    halo_send,
+    halo_recv,
+    send_sem,
+    recv_sem,
+    local_sem,
+    out_sem,
+):
+    ways = lax.axis_size("dp")
+    members = lax.axis_size("seq")
+    chips = ways // 2
+    me = lax.axis_index("dp")
+    place = lax.axis_index("seq")
+    chip = me // 2
+    core = me % 2
+    partner = chip * 2 + 1 - core
+    count = tok_ref.shape[0]
+    _, row_parts, column_parts, _, _, columns = conv_full.shape
+    depth = conv_full.shape[4]
+
+    def peer_of(step):
+        return (chip + step) % chips * 2 + core
+
+    barrier = pltpu.get_barrier_semaphore()
+    pl.semaphore_signal(barrier, inc=1, device_id=(partner, place), device_id_type=MESH)
+    for step in range(1, chips):
+        pl.semaphore_signal(
+            barrier, inc=1, device_id=(peer_of(step), place), device_id_type=MESH
+        )
+    for turn in range(1, members):
+        pl.semaphore_signal(
+            barrier, inc=1, device_id=(me, (place + turn) % members), device_id_type=MESH
+        )
+    pl.semaphore_wait(barrier, 1 + (chips - 1) + (members - 1))
+
+    right = (place + 1) % members
+    left = (place + members - 1) % members
+    halo = [
+        pltpu.make_async_remote_copy(
+            tok_ref.at[count - 8 : count], low_ref, halo_send.at[0], halo_recv.at[0], (me, right), MESH
+        ),
+        pltpu.make_async_remote_copy(
+            tok_ref.at[0:8], high_ref, halo_send.at[1], halo_recv.at[1], (me, left), MESH
+        ),
+    ]
+    for copy in halo:
+        copy.start()
+
+    def conv_source(spot):
+        rows = pl.multiple_of(spot // column_parts * depth, depth)
+        at = pl.multiple_of(spot % column_parts * columns, columns)
+        return conv_ref.at[:, pl.ds(rows, depth), pl.ds(at, columns)]
+
+    def conv_slot(way, spot):
+        return conv_full.at[way, spot // column_parts, spot % column_parts]
+
+    def attn_source(spot):
+        return attn_ref.at[spot]
+
+    def attn_slot(way, spot):
+        return attn_full.at[way, spot]
+
+    kinds = ((conv_source, conv_slot), (attn_source, attn_slot))
+    sent = ([], [])
+    local = ([], [])
+
+    def send(kind, source, way, spot, target):
+        copy = pltpu.make_async_remote_copy(
+            source,
+            kinds[kind][1](way, spot),
+            send_sem.at[kind, len(sent[kind])],
+            recv_sem.at[kind, way, spot],
+            target,
+            MESH,
+        )
+        copy.start()
+        sent[kind].append(copy)
+
+    def arrived(kind, way, spot):
+        slot = kinds[kind][1](way, spot)
+        pltpu.make_async_remote_copy(
+            slot, slot, send_sem.at[kind, 0], recv_sem.at[kind, way, spot], (partner, place), MESH
+        ).wait_recv()
+
+    def first(kind):
+        source, slot = kinds[kind]
+        for step in range(1, chips):
+            send(kind, source(place), me, place, (peer_of(step), place))
+        for spot in range(members):
+            send(kind, source(spot), me, spot, (partner, place))
+            copy = pltpu.make_async_copy(source(spot), slot(me, spot), local_sem.at[kind, spot])
+            copy.start()
+            local[kind].append(copy)
+
+    order = sorted(range(1, chips), key=lambda step: min(step, chips - step))
+
+    def second(kind):
+        slot = kinds[kind][1]
+        for step in order:
+            way = peer_of(step)
+            arrived(kind, way, place)
+            for turn in range(1, members):
+                send(kind, slot(way, place), way, place, (me, (place + turn) % members))
+            send(kind, slot(way, place), way, place, (partner, place))
+
+    def third(kind):
+        slot = kinds[kind][1]
+        for step in order:
+            way = peer_of(step)
+            for turn in range(1, members):
+                spot = (place + turn) % members
+                arrived(kind, way, spot)
+                send(kind, slot(way, spot), way, spot, (partner, place))
+
+    def finish(kind):
+        for step in range(chips):
+            way = (chip + step) % chips * 2 + 1 - core
+            for spot in range(members):
+                arrived(kind, way, spot)
+        for copy in local[kind]:
+            copy.wait()
+        for copy in sent[kind]:
+            copy.wait_send()
+
+    first(0)
+    for copy in halo:
+        copy.wait()
+    low = jnp.where(place > 0, low_ref[7:8], 0)
+    high = jnp.where(place < members - 1, high_ref[0:1], 0)
+    stem_compute(
+        tok_ref,
+        low,
+        high,
+        stem_weight_ref,
+        stem_bias_ref,
+        gain_ref,
+        ext_ref,
+        text_ref,
+        hot_ref,
+        shifted_ref,
+        rows_ref,
+    )
+    second(0)
+    first(1)
+    third(0)
+    finish(0)
+
+    width = 256
+    steps = columns // width
+    group = 4
+    channels = ext_ref.shape[1]
+    big = jnp.full((count, width), jnp.finfo(jnp.float32).max, jnp.float32)
+
+    def panel(index, nothing):
+        b = index // steps
+        inner = pl.multiple_of(index % steps * width, width)
+
+        def block(m, carry):
+            most, least = carry
+            total = None
+            for tap in range(KW):
+                start = pl.multiple_of((m * group + tap) * count, count)
+                part = jnp.dot(
+                    ext_ref[pl.ds(start, group * count), :],
+                    conv_full[:, :, b, tap, :, pl.ds(inner, width)].reshape(channels, width),
+                    preferred_element_type=jnp.float32,
+                )
+                total = part if total is None else total + part
+            for piece_index in range(group):
+                piece = total[piece_index * count : (piece_index + 1) * count]
+                most = jnp.maximum(most, piece)
+                least = jnp.minimum(least, piece)
+            return most, least
+
+        most, least = lax.fori_loop(0, POOL_B // group, block, (-big, big))
+        at = pl.multiple_of(index * width, width)
+        bias = conv_bias_ref[:, pl.ds(at, width)]
+        coarse_ref[:, pl.ds(at, width)] = jnp.maximum(
+            jax.nn.gelu(most + bias), jax.nn.gelu(least + bias)
+        ).astype(jnp.bfloat16)
+        return nothing
+
+    panels = column_parts * steps
+    early = panels // 3
+    lax.fori_loop(0, early, panel, 0)
+    second(1)
+    lax.fori_loop(early, panels, panel, 0)
+    third(1)
+    finish(1)
+    out = pltpu.make_async_copy(attn_full, full_attn_ref, out_sem)
+    out.start()
+    out.wait()
+
+
+def row_parts_of(depth, columns, members):
+    for row_parts in (2, 1, 3):
+        column_parts = members // row_parts
+        if members % row_parts or depth % (16 * row_parts) or columns % (256 * column_parts):
+            continue
+        return row_parts, column_parts
+    return None
+
+
+def encoder_stage(tokens, stem_weight, stem_bias, conv_gain, conv_bias, conv_weight, attn_rows, parts):
+    count = tokens.shape[0]
+    channels = stem_weight.shape[1]
+    taps, depth, columns = conv_weight.shape
+    ways = lax.axis_size("dp")
+    members = lax.axis_size("seq")
+    row_parts, column_parts = parts
+    copies = (ways // 2 - 1) * (2 * members) + members + ways
+    full_attn = (ways,) + attn_rows.shape
+    vmem = pl.BlockSpec(memory_space=pltpu.VMEM)
+    hbm = pl.BlockSpec(memory_space=pl.ANY)
+    return pl.pallas_call(
+        encoder_kernel,
+        out_shape=(
+            jax.ShapeDtypeStruct((count, columns), jnp.bfloat16),
+            jax.ShapeDtypeStruct(full_attn, jnp.bfloat16),
+        ),
+        in_specs=[vmem] * 5 + [hbm] * 2,
+        out_specs=(vmem, hbm),
+        scratch_shapes=[
+            pltpu.VMEM((GROUP + 2 * SPAN, count), jnp.float32),
+            pltpu.VMEM((POOL_B + 1, count, GROUP), jnp.bfloat16),
+            pltpu.VMEM((POOL_A, GROUP, channels), jnp.bfloat16),
+            pltpu.VMEM((count, channels), jnp.float32),
+            pltpu.VMEM(((POOL_B + 4) * count, channels), jnp.bfloat16),
+            pltpu.VMEM((8, GROUP), jnp.int32),
+            pltpu.VMEM((8, GROUP), jnp.int32),
+            pltpu.VMEM(
+                (ways, row_parts, column_parts, taps, depth // row_parts, columns // column_parts),
+                jnp.bfloat16,
+            ),
+            pltpu.VMEM(full_attn, jnp.bfloat16),
+            pltpu.SemaphoreType.DMA((2,)),
+            pltpu.SemaphoreType.DMA((2,)),
+            pltpu.SemaphoreType.DMA((2, copies)),
+            pltpu.SemaphoreType.DMA((2, ways, members)),
+            pltpu.SemaphoreType.DMA((2, members)),
+            pltpu.SemaphoreType.DMA(()),
+        ],
+        compiler_params=pltpu.CompilerParams(
+            collective_id=0, has_side_effects=True, vmem_limit_bytes=56 * 2**20
+        ),
+        name="encoder_stage",
+    )(tokens, stem_weight, stem_bias[None], conv_gain[None], conv_bias[None], conv_weight, attn_rows)
+
+
 def gather_conv(conv_weight):
     taps, depth, columns = conv_weight.shape
     members = lax.axis_size("seq")
@@ -241,24 +529,47 @@
 ):
     seq_local = tokens.shape[1]
     rows_att = seq_local // GROUP
-    full_conv = gather_conv(conv_weight)
-    projections = gather_rows(jnp.concatenate([w_query, w_key, w_value], axis=1))
-    full_out = gather_rows(w_out)
     tokens = tokens.reshape(rows_att, GROUP)
     size = lax.axis_size("seq")
-    forward = [(i, i + 1) for i in range(size - 1)]
-    backward = [(i + 1, i) for i in range(size - 1)]
-    low = lax.ppermute(tokens[-1:], "seq", forward)
-    high = lax.ppermute(tokens[:1], "seq", backward)
-    ext = stem_stage(tokens, low, high, stem_weight, stem_bias, conv_gain)
-    coarse = conv_stage(ext, full_conv, conv_bias)
+    rows = w_out.shape[0]
+    parts = row_parts_of(conv_weight.shape[1], conv_weight.shape[2], size)
+    split = HEADS * HEAD_K
+    if parts is not None and rows % (16 * size) == 0:
+        packed = jnp.concatenate([w_query, w_key, w_out, w_value], axis=1)
+        coarse, full = encoder_stage(
+            tokens,
+            stem_weight,
+            stem_bias,
+            conv_gain,
+            conv_bias,
+            conv_weight,
+            packed.reshape(size, rows // size, -1),
+            parts,
+        )
+        full = full.reshape(-1, full.shape[-1])
+        middle = split + HEAD_K
+        wide = w_out.shape[1]
+        first_rows = full[:, :middle]
+        value_rows = full[:, middle + wide :]
+        full_out = full[:, middle : middle + wide]
+    else:
+        full_conv = gather_conv(conv_weight)
+        projections = gather_rows(jnp.concatenate([w_query, w_key, w_value], axis=1))
+        first_rows = projections[:, : split + HEAD_K]
+        value_rows = projections[:, split + HEAD_K :]
+        full_out = gather_rows(w_out)
+        forward = [(i, i + 1) for i in range(size - 1)]
+        backward = [(i + 1, i) for i in range(size - 1)]
+        low = lax.ppermute(tokens[-1:], "seq", forward)
+        high = lax.ppermute(tokens[:1], "seq", backward)
+        ext = stem_stage(tokens, low, high, stem_weight, stem_bias, conv_gain)
+        coarse = conv_stage(ext, full_conv, conv_bias)
     residual = coarse.astype(jnp.float32)
     hidden = rms_scale(residual, attn_gain).astype(jnp.bfloat16)
-    projected = jnp.dot(hidden, projections, preferred_element_type=jnp.float32)
-    split = HEADS * HEAD_K
+    projected = jnp.dot(hidden, first_rows, preferred_element_type=jnp.float32)
     query = projected[:, :split]
-    keys = projected[:, split : split + HEAD_K]
-    values = projected[:, split + HEAD_K :]
+    keys = projected[:, split:]
+    values = jnp.dot(hidden, value_rows, preferred_element_type=jnp.float32)
     half_dim = HEAD_K // 2
     freqs = 10000.0 ** (-jnp.arange(half_dim, dtype=jnp.float32) / half_dim)
     positions = lax.axis_index("seq") * rows_att + jnp.arange(rows_att, dtype=jnp.int32)

time: 244 us -> 174 us (0.71)
  waiting for transfers between devices: 142 us -> 0 us
  Pallas kernels: 48.6 us -> 144 us
  between operations: 13.3 us -> 0.1 us
  starting transfers between devices: 4.79 us -> 0 us
  local copies, waits for them, and re-layouts: 8.71 us -> 4.72 us
    all_gather x3 -> x0, waiting for transfers between devices: 139 us -> none  [the longest x2 74.1 us: gather_rows(): return lax.all_gather(piece, ('dp', 'seq'), axis=0, tiled=True)]
    pallas_call x2 -> x1, Pallas kernels: 48.6 us -> 144 us  [encoder_stage(): pl.pallas_call(encoder_kernel, out_shape=(jax.ShapeDtypeStruct((count, co...]
    ppermute x2 -> x0, starting transfers between devices: 4.68 us -> none  [the longest x1 3.38 us: body(): low = lax.ppermute(tokens[-1:], 'seq', forward)]
    unnamed x20 -> x8, local copies, waits for them, and re-layouts: 3.62 us -> 0.42 us
  transfers between devices with their start and end apart: 5 -> 0, of which waited for: 4 -> 0; matrix products, arithmetic and copies ran while one was open for 7% -> 0% of each run, Pallas kernels for 20% -> 0%
where the time goes in v2:
time: 174 us; the launch traced here: 173 us
  Pallas kernels  144 us (83%)
  matrix products  9.81 us (6%)
  blocking collectives  9.67 us (6%)
  local copies, waits for them, and re-layouts  4.72 us (3%)
  other arithmetic  4.56 us (3%)
    pallas_call x1, Pallas kernels, encoder_stage(): pl.pallas_call(encoder_kernel, out_shape=(jax.ShapeDtypeStruct((count, co...  144 us
    all_gather x1, blocking collectives, body(): pair = lax.all_gather(pair, 'seq', axis=0, tiled=True)  9.67 us
    dot_general x1, matrix products, body(): out = jnp.dot(mixed, full_out, preferred_element_type=jnp.float32)  3.89 us

profile of v2, /device:TPU:8, one launch (start us, length us, event | category | flops | bytes accessed | tf_op | source)
XLA Modules:
  0.0 173.3 jit_solution(2988545981501464184)
XLA Ops:
  0.0 1.3 broadcast_in_dim.8.stem_bias_ref
  1.3 1.3 broadcast_in_dim.9.gain_ref
  2.6 1.3 broadcast_in_dim.10.conv_bias_ref
  3.9 2.3 %pad_maximum_fusion = bf16[192,2880]{1,0:T(8,128)(2,1)} fusion(bf16[192,192]{1,0:T(8,128)(2,1)} %param.20, bf16[192,1536]{1,0:T(8,128)(2,1)} %param.21, bf16[192,128]{1,0:T(8,128)(2,1)} %param.19, bf16[192,1024]{1,0:T(8,128)(2,1)} %param.18), kind=kLoop, calls=%fused_computation.17 | loop fusion | flops 4423680 | bytes 2211840 | tf_op jit(solution)/shard_map/concatenate | solution.py:538
  6.2 0.0 copy-start.1
  6.2 144.5 %encoder_stage.1 = (bf16[128,1536]{1,0:T(8,128)(2,1)}, bf16[8,4,48,2880]{3,2,1,0:T(8,128)(2,1)}) custom-call(s32[128,128]{1,0:T(8,128)} %bitcast.39, bf16[60,768]{1,0:T(8,128)(2,1)} %stem_weight_ref.1, f32[1,768]{1,0:T(1,128)} %broadcast_in_dim.8.stem_bias_ref, f32[1,768]{1,0:T(1,128)} %broadcast_in_dim.9.gain_ref, ...), custom_call_target="tpu_custom_call" | custom-call | tf_op jit(solution)/shard_map/encoder_stage/pallas_call | solution.py:454
  150.7 1.2 fusion.20
  151.8 0.0 copy-done.1
  151.9 1.7 convolution_convert_fusion.1
  153.6 2.9 %fusion.3 = f32[128,1152]{1,0:T(8,128)S(1)} fusion(bf16[1536,2880]{1,0:T(8,128)(2,1)} %bitcast.41, bf16[128,1536]{1,0:T(8,128)(2,1)} %get-tuple-element.7, f32[1536]{0:T(1024)S(1)} %copy-done.1, f32[128]{0:T(128)S(1)} %add_rsqrt_fusion), kind=kOutput, calls=%fused_computation.3 | convolution fusion | flops 453771264 | bytes 4528640 | tf_op jit(solution)/shard_map/dot_general | solution.py:569
  156.4 0.1 fusion.39
  156.5 0.1 slice_bitcast_fusion
  156.6 0.1 copy.33
  156.7 0.1 copy.30
  156.7 0.1 copy.29
  156.8 0.2 subtract_convert_fusion.1
  157.1 0.1 copy.23
  157.1 0.1 copy.21
  157.2 9.7 %all_gather.3 = bf16[512,320]{0,1:T(8,128)(2,1)S(1)} all-gather(bf16[128,320]{0,1:T(8,128)(2,1)S(1)} %pad_maximum_fusion.1), channel_id=1, replica_groups=mesh['dp'=8,'seq'=4] {'seq'}, dimensions={0}, use_global_device_ids=true | all-gather | bytes 409600 | tf_op jit(solution)/shard_map/all_gather | solution.py:580
  166.9 0.2 fusion.40
  167.1 0.2 subtract_convert_fusion
  167.3 0.5 fusion.24
  167.9 0.6 fusion.41
  168.4 0.0 copy-start
  168.5 0.9 convolution_convert_fusion
  169.3 0.1 copy-done
  169.4 3.9 %fusion.11 = bf16[1,128,1536]{2,1,0:T(8,128)(2,1)} fusion(bf16[128,1536]{0,1:T(8,128)(2,1)S(1)} %bitcast.43, bf16[1536,2880]{1,0:T(8,128)(2,1)} %bitcast.42, bf16[128,1536]{1,0:T(8,128)(2,1)S(1)} %copy-done), kind=kOutput, calls=%fused_computation.7 | convolution fusion | flops 604569600 | bytes 5898240 | tf_op jit(solution)/shard_map/dot_general | solution.py:590
  (4 shorter events, 0.0 us)
Async XLA Ops:
  6.2 145.7 %copy-start.1 = (f32[1536]{0:T(1024)S(1)}, f32[1536]{0:T(1024)}, u32[]{:S(2)}) copy-start(f32[1536]{0:T(1024)} %param.17) | copy-start | bytes 18436
  168.4 1.0 copy-start

commit v3 on v2

--- a/solution.py
+++ b/solution.py
@@ -54,7 +54,7 @@
 
 
 def stem_compute(
-    tok_ref, low, high, weight_ref, bias_ref, gain_ref, ext_ref, text_ref, hot_ref, shifted_ref, rows_ref
+    tok_ref, low, high, weight_ref, bias_ref, gain_ref, ext_ref, text_ref, hot_ref, shifted_ref, rows_ref, between=None
 ):
     count = tok_ref.shape[0]
     channels = weight_ref.shape[1]
@@ -122,7 +122,12 @@
         ext_ref[pl.ds(start, count), :] = rms_scale(pooled, gain_ref[...]).astype(jnp.bfloat16)
         return carry
 
-    lax.fori_loop(0, POOL_B + 1, block, 0)
+    if between is None:
+        lax.fori_loop(0, POOL_B + 1, block, 0)
+    else:
+        lax.fori_loop(0, POOL_B // 2, block, 0)
+        between()
+        lax.fori_loop(POOL_B // 2, POOL_B + 1, block, 0)
     edges = ext_ref[(POOL_B + 2) * count : (POOL_B + 3) * count, :].astype(jnp.float32)
     left_keep = (place > 0).astype(jnp.float32)
     right_keep = (place < last_place).astype(jnp.float32)
@@ -242,6 +247,7 @@
     halo_recv,
     send_sem,
     recv_sem,
+    half_sem,
     local_sem,
     out_sem,
 ):
@@ -299,7 +305,22 @@
     def attn_slot(way, spot):
         return attn_full.at[way, spot]
 
-    kinds = ((conv_source, conv_slot), (attn_source, attn_slot))
+    def conv_half(way, spot, half, turn):
+        cut = columns // 256 * 128
+        where = pl.ds(0, cut) if half == 0 else pl.ds(cut, columns - cut)
+        return conv_full.at[way, spot // column_parts, spot % column_parts, :, :, where]
+
+    def attn_half(way, spot, half, turn):
+        rows = attn_ref.shape[1]
+        tiles = rows // 16
+        cut = (tiles // 2 if turn % 2 else tiles - tiles // 2) * 16
+        where = pl.ds(0, cut) if half == 0 else pl.ds(cut, rows - cut)
+        return attn_full.at[way, spot, where]
+
+    kinds = ((conv_source, conv_slot, conv_half), (attn_source, attn_slot, attn_half))
+    along_x = place + 1 - 2 * (place % 2)
+    along_y = place + 2 - 4 * (place // 2)
+    across = 3 - place
     sent = ([], [])
     local = ([], [])
 
@@ -322,7 +343,7 @@
         ).wait_recv()
 
     def first(kind):
-        source, slot = kinds[kind]
+        source, slot, _ = kinds[kind]
         for step in range(1, chips):
             send(kind, source(place), me, place, (peer_of(step), place))
         for spot in range(members):
@@ -333,23 +354,49 @@
 
     order = sorted(range(1, chips), key=lambda step: min(step, chips - step))
 
-    def second(kind):
+    def second(kind, some):
         slot = kinds[kind][1]
-        for step in order:
+        for step in some:
             way = peer_of(step)
             arrived(kind, way, place)
-            for turn in range(1, members):
-                send(kind, slot(way, place), way, place, (me, (place + turn) % members))
+            send(kind, slot(way, place), way, place, (me, along_x))
+            send(kind, slot(way, place), way, place, (me, along_y))
             send(kind, slot(way, place), way, place, (partner, place))
+
+    def send_half(kind, way, spot, half, turn, target):
+        ref = kinds[kind][2](way, spot, half, turn)
+        copy = pltpu.make_async_remote_copy(
+            ref,
+            ref,
+            send_sem.at[kind, len(sent[kind])],
+            half_sem.at[kind, way, half],
+            (me, target),
+            MESH,
+        )
+        copy.start()
+        sent[kind].append(copy)
 
     def third(kind):
         slot = kinds[kind][1]
-        for step in order:
+        for turn, step in enumerate(order):
             way = peer_of(step)
-            for turn in range(1, members):
-                spot = (place + turn) % members
-                arrived(kind, way, spot)
-                send(kind, slot(way, spot), way, spot, (partner, place))
+            arrived(kind, way, along_x)
+            send_half(kind, way, along_x, 0, turn, along_y)
+            send(kind, slot(way, along_x), way, along_x, (partner, place))
+            arrived(kind, way, along_y)
+            send_half(kind, way, along_y, 1, turn, along_x)
+            send(kind, slot(way, along_y), way, along_y, (partner, place))
+
+    def fourth(kind):
+        slot, half_of = kinds[kind][1:]
+        for turn, step in enumerate(order):
+            way = peer_of(step)
+            for half in range(2):
+                ref = half_of(way, across, half, turn)
+                pltpu.make_async_remote_copy(
+                    ref, ref, send_sem.at[kind, 0], half_sem.at[kind, way, half], (partner, place), MESH
+                ).wait_recv()
+            send(kind, slot(way, across), way, across, (partner, place))
 
     def finish(kind):
         for step in range(chips):
@@ -378,10 +425,14 @@
         hot_ref,
         shifted_ref,
         rows_ref,
+        lambda: second(0, order[:1]),
     )
-    second(0)
+    second(0, order[1:])
     first(1)
     third(0)
+    second(1, order[:1])
+    fourth(0)
+    second(1, order[1:])
     finish(0)
 
     width = 256
@@ -420,11 +471,11 @@
         return nothing
 
     panels = column_parts * steps
-    early = panels // 3
+    early = panels // 2
     lax.fori_loop(0, early, panel, 0)
-    second(1)
+    third(1)
     lax.fori_loop(early, panels, panel, 0)
-    third(1)
+    fourth(1)
     finish(1)
     out = pltpu.make_async_copy(attn_full, full_attn_ref, out_sem)
     out.start()
@@ -476,6 +527,7 @@
             pltpu.SemaphoreType.DMA((2,)),
             pltpu.SemaphoreType.DMA((2, copies)),
             pltpu.SemaphoreType.DMA((2, ways, members)),
+            pltpu.SemaphoreType.DMA((2, ways, 2)),
             pltpu.SemaphoreType.DMA((2, members)),
             pltpu.SemaphoreType.DMA(()),
         ],
@@ -534,7 +586,7 @@
     rows = w_out.shape[0]
     parts = row_parts_of(conv_weight.shape[1], conv_weight.shape[2], size)
     split = HEADS * HEAD_K
-    if parts is not None and rows % (16 * size) == 0:
+    if size == 4 and parts is not None and rows % (16 * size) == 0:
         packed = jnp.concatenate([w_query, w_key, w_out, w_value], axis=1)
         coarse, full = encoder_stage(
             tokens,

time: 174 us -> 144 us (0.83)
  Pallas kernels: 144 us -> 114 us
    pallas_call x1, Pallas kernels: 144 us -> 114 us  [encoder_stage(): pl.pallas_call(encoder_kernel, out_shape=(jax.ShapeDtypeStruct((count, co...]
where the time goes in v3:
time: 144 us; the launch traced here: 143 us
  Pallas kernels  114 us (79%)
  matrix products  9.81 us (7%)
  blocking collectives  9.76 us (7%)
  local copies, waits for them, and re-layouts  4.73 us (3%)
  other arithmetic  4.56 us (3%)
    pallas_call x1, Pallas kernels, encoder_stage(): pl.pallas_call(encoder_kernel, out_shape=(jax.ShapeDtypeStruct((count, co...  114 us
    all_gather x1, blocking collectives, body(): pair = lax.all_gather(pair, 'seq', axis=0, tiled=True)  9.76 us
    dot_general x1, matrix products, body(): out = jnp.dot(mixed, full_out, preferred_element_type=jnp.float32)  3.9 us

profile of v3, /device:TPU:8, one launch (start us, length us, event | category | flops | bytes accessed | tf_op | source)
XLA Modules:
  0.0 143.2 jit_solution(16348374514372938574)
XLA Ops:
  0.0 1.3 broadcast_in_dim.8.stem_bias_ref
  1.3 1.3 broadcast_in_dim.9.gain_ref
  2.6 1.3 broadcast_in_dim.10.conv_bias_ref
  3.9 2.3 %pad_maximum_fusion = bf16[192,2880]{1,0:T(8,128)(2,1)} fusion(bf16[192,192]{1,0:T(8,128)(2,1)} %param.20, bf16[192,1536]{1,0:T(8,128)(2,1)} %param.21, bf16[192,128]{1,0:T(8,128)(2,1)} %param.19, bf16[192,1024]{1,0:T(8,128)(2,1)} %param.18), kind=kLoop, calls=%fused_computation.17 | loop fusion | flops 4423680 | bytes 2211840 | tf_op jit(solution)/shard_map/concatenate | solution.py:590
  6.2 0.0 copy-start.1
  6.2 114.2 %encoder_stage.1 = (bf16[128,1536]{1,0:T(8,128)(2,1)}, bf16[8,4,48,2880]{3,2,1,0:T(8,128)(2,1)}) custom-call(s32[128,128]{1,0:T(8,128)} %bitcast.39, bf16[60,768]{1,0:T(8,128)(2,1)} %stem_weight_ref.1, f32[1,768]{1,0:T(1,128)} %broadcast_in_dim.8.stem_bias_ref, f32[1,768]{1,0:T(1,128)} %broadcast_in_dim.9.gain_ref, ...), custom_call_target="tpu_custom_call" | custom-call | tf_op jit(solution)/shard_map/encoder_stage/pallas_call | solution.py:505
  120.4 1.2 fusion.20
  121.6 0.0 copy-done.1
  121.6 1.7 %convolution_convert_fusion.1 = bf16[128,192]{0,1:T(8,128)(2,1)S(1)} fusion(bf16[1536,2880]{1,0:T(8,128)(2,1)} %bitcast.40, bf16[128,1536]{1,0:T(8,128)(2,1)} %get-tuple-element.7, f32[1536]{0:T(1024)S(1)} %copy-done.1, f32[128]{0:T(128)S(1)} %add_rsqrt_fusion), kind=kOutput, calls=%fused_computation.18 | convolution fusion | flops 76308480 | bytes 1235456 | tf_op jit(solution)/shard_map/dot_general | solution.py:624
  123.3 2.9 %fusion.3 = f32[128,1152]{1,0:T(8,128)S(1)} fusion(bf16[1536,2880]{1,0:T(8,128)(2,1)} %bitcast.41, bf16[128,1536]{1,0:T(8,128)(2,1)} %get-tuple-element.7, f32[1536]{0:T(1024)S(1)} %copy-done.1, f32[128]{0:T(128)S(1)} %add_rsqrt_fusion), kind=kOutput, calls=%fused_computation.3 | convolution fusion | flops 453771264 | bytes 4528640 | tf_op jit(solution)/shard_map/dot_general | solution.py:621
  126.1 0.1 fusion.39
  126.2 0.1 slice_bitcast_fusion
  126.3 0.1 copy.33
  126.4 0.1 copy.30
  126.5 0.1 copy.29
  126.5 0.2 subtract_convert_fusion.1
  126.8 0.1 copy.23
  126.9 0.1 copy.21
  127.0 9.8 %all_gather.3 = bf16[512,320]{0,1:T(8,128)(2,1)S(1)} all-gather(bf16[128,320]{0,1:T(8,128)(2,1)S(1)} %pad_maximum_fusion.1), channel_id=1, replica_groups=mesh['dp'=8,'seq'=4] {'seq'}, dimensions={0}, use_global_device_ids=true | all-gather | bytes 409600 | tf_op jit(solution)/shard_map/all_gather | solution.py:632
  136.7 0.2 fusion.40
  136.9 0.2 subtract_convert_fusion
  137.2 0.5 fusion.24
  137.7 0.6 fusion.41
  138.3 0.0 copy-start
  138.3 0.9 convolution_convert_fusion
  139.1 0.1 copy-done
  139.3 3.9 %fusion.11 = bf16[1,128,1536]{2,1,0:T(8,128)(2,1)} fusion(bf16[128,1536]{0,1:T(8,128)(2,1)S(1)} %bitcast.43, bf16[1536,2880]{1,0:T(8,128)(2,1)} %bitcast.42, bf16[128,1536]{1,0:T(8,128)(2,1)S(1)} %copy-done), kind=kOutput, calls=%fused_computation.7 | convolution fusion | flops 604569600 | bytes 5898240 | tf_op jit(solution)/shard_map/dot_general | solution.py:642
  (4 shorter events, 0.0 us)
Async XLA Ops:
  6.2 115.4 %copy-start.1 = (f32[1536]{0:T(1024)S(1)}, f32[1536]{0:T(1024)}, u32[]{:S(2)}) copy-start(f32[1536]{0:T(1024)} %param.17) | copy-start | bytes 18436
  138.3 1.0 copy-start

commit v4 on v3

--- a/solution.py
+++ b/solution.py
@@ -227,13 +227,17 @@
 def encoder_kernel(
     tok_ref,
     stem_weight_ref,
-    stem_bias_ref,
-    gain_ref,
-    conv_bias_ref,
+    vector_ref,
+    cosine_ref,
+    sine_ref,
     conv_ref,
     attn_ref,
+    out_ref,
     coarse_ref,
-    full_attn_ref,
+    key_ref,
+    value_ref,
+    pair_send,
+    pair_recv,
     text_ref,
     hot_ref,
     shifted_ref,
@@ -249,8 +253,13 @@
     recv_sem,
     half_sem,
     local_sem,
-    out_sem,
 ):
+    stem_wide = stem_weight_ref.shape[1]
+    wide = out_ref.shape[1]
+    stem_bias_ref = vector_ref.at[:, 0:stem_wide]
+    gain_ref = vector_ref.at[:, stem_wide : 2 * stem_wide]
+    conv_bias_ref = vector_ref.at[:, 2 * stem_wide : 2 * stem_wide + wide]
+    attn_gain_ref = vector_ref.at[:, 2 * stem_wide + wide :]
     ways = lax.axis_size("dp")
     members = lax.axis_size("seq")
     chips = ways // 2
@@ -477,9 +486,73 @@
     lax.fori_loop(early, panels, panel, 0)
     fourth(1)
     finish(1)
-    out = pltpu.make_async_copy(attn_full, full_attn_ref, out_sem)
-    out.start()
-    out.wait()
+    split = HEADS * HEAD_K
+    middle = split + HEAD_K
+
+    def weight(begin, end):
+        return attn_full[:, :, :, begin:end].reshape(wide, end - begin)
+
+    def turned(head):
+        return (
+            head * cosine_ref[...] + pltpu.roll(head, HEAD_K // 2, 1) * sine_ref[...]
+        ).astype(jnp.bfloat16)
+
+    hidden = rms_scale(coarse_ref[...].astype(jnp.float32), attn_gain_ref[...]).astype(
+        jnp.bfloat16
+    )
+    key_ref[place] = turned(
+        jnp.dot(hidden, weight(split, middle), preferred_element_type=jnp.float32)
+    )
+    value_ref[place] = jnp.dot(
+        hidden, weight(middle + wide, middle + wide + HEAD_V), preferred_element_type=jnp.float32
+    ).astype(jnp.bfloat16)
+    pairs = []
+    for turn in range(1, members):
+        for index, ref in enumerate((key_ref, value_ref)):
+            copy = pltpu.make_async_remote_copy(
+                ref.at[place],
+                ref.at[place],
+                pair_send.at[index, turn],
+                pair_recv.at[index, place],
+                (me, (place + turn) % members),
+                MESH,
+            )
+            copy.start()
+            pairs.append(copy)
+    query = jnp.dot(hidden, weight(0, split), preferred_element_type=jnp.float32)
+    for turn in range(1, members):
+        spot = (place + turn) % members
+        for index, ref in enumerate((key_ref, value_ref)):
+            pltpu.make_async_remote_copy(
+                ref.at[spot],
+                ref.at[spot],
+                pair_send.at[index, 0],
+                pair_recv.at[index, spot],
+                (partner, place),
+                MESH,
+            ).wait_recv()
+    keys = key_ref[...].reshape(members * count, HEAD_K)
+    values = value_ref[...].reshape(members * count, HEAD_V)
+    projection = weight(middle, middle + wide)
+    total = coarse_ref[...].astype(jnp.float32)
+    for head in range(HEADS):
+        scores = lax.dot_general(
+            turned(query[:, head * HEAD_K : (head + 1) * HEAD_K]),
+            keys,
+            (((1,), (1,)), ((), ())),
+            preferred_element_type=jnp.float32,
+        ) * HEAD_K ** (-0.5)
+        raised = jnp.exp(scores - jnp.max(scores, axis=-1, keepdims=True))
+        weights = (raised / jnp.sum(raised, axis=-1, keepdims=True)).astype(jnp.bfloat16)
+        mixed = jnp.dot(weights, values, preferred_element_type=jnp.float32).astype(jnp.bfloat16)
+        total = total + jnp.dot(
+            mixed,
+            projection[head * HEAD_V : (head + 1) * HEAD_V],
+            preferred_element_type=jnp.float32,
+        )
+    out_ref[...] = total.astype(jnp.bfloat16)
+    for copy in pairs:
+        copy.wait_send()
 
 
 def row_parts_of(depth, columns, members):
@@ -491,7 +564,7 @@
     return None
 
 
-def encoder_stage(tokens, stem_weight, stem_bias, conv_gain, conv_bias, conv_weight, attn_rows, parts):
+def encoder_stage(tokens, stem_weight, vectors, cosine, sine, conv_weight, attn_rows, parts):
     count = tokens.shape[0]
     channels = stem_weight.shape[1]
     taps, depth, columns = conv_weight.shape
@@ -504,13 +577,15 @@
     hbm = pl.BlockSpec(memory_space=pl.ANY)
     return pl.pallas_call(
         encoder_kernel,
-        out_shape=(
-            jax.ShapeDtypeStruct((count, columns), jnp.bfloat16),
-            jax.ShapeDtypeStruct(full_attn, jnp.bfloat16),
-        ),
+        out_shape=jax.ShapeDtypeStruct((count, columns), jnp.bfloat16),
         in_specs=[vmem] * 5 + [hbm] * 2,
-        out_specs=(vmem, hbm),
+        out_specs=vmem,
         scratch_shapes=[
+            pltpu.VMEM((count, columns), jnp.bfloat16),
+            pltpu.VMEM((members, count, HEAD_K), jnp.bfloat16),
+            pltpu.VMEM((members, count, HEAD_V), jnp.bfloat16),
+            pltpu.SemaphoreType.DMA((2, members)),
+            pltpu.SemaphoreType.DMA((2, members)),
             pltpu.VMEM((GROUP + 2 * SPAN, count), jnp.float32),
             pltpu.VMEM((POOL_B + 1, count, GROUP), jnp.bfloat16),
             pltpu.VMEM((POOL_A, GROUP, channels), jnp.bfloat16),
@@ -529,13 +604,12 @@
             pltpu.SemaphoreType.DMA((2, ways, members)),
             pltpu.SemaphoreType.DMA((2, ways, 2)),
             pltpu.SemaphoreType.DMA((2, members)),
-            pltpu.SemaphoreType.DMA(()),
         ],
         compiler_params=pltpu.CompilerParams(
             collective_id=0, has_side_effects=True, vmem_limit_bytes=56 * 2**20
         ),
         name="encoder_stage",
-    )(tokens, stem_weight, stem_bias[None], conv_gain[None], conv_bias[None], conv_weight, attn_rows)
+    )(tokens, stem_weight, vectors[None], cosine, sine, conv_weight, attn_rows)
 
 
 def gather_conv(conv_weight):
@@ -588,22 +662,21 @@
     split = HEADS * HEAD_K
     if size == 4 and parts is not None and rows % (16 * size) == 0:
         packed = jnp.concatenate([w_query, w_key, w_out, w_value], axis=1)
-        coarse, full = encoder_stage(
+        half_dim = HEAD_K // 2
+        freqs = 10000.0 ** (-jnp.arange(half_dim, dtype=jnp.float32) / half_dim)
+        positions = lax.axis_index("seq") * rows_att + jnp.arange(rows_att, dtype=jnp.int32)
+        angles = positions.astype(jnp.float32)[:, None] * freqs[None, :]
+        cosine, sine = jnp.cos(angles), jnp.sin(angles)
+        return encoder_stage(
             tokens,
             stem_weight,
-            stem_bias,
-            conv_gain,
-            conv_bias,
+            jnp.concatenate([stem_bias, conv_gain, conv_bias, attn_gain]),
+            jnp.concatenate([cosine, cosine], axis=1),
+            jnp.concatenate([-sine, sine], axis=1),
             conv_weight,
             packed.reshape(size, rows // size, -1),
             parts,
-        )
-        full = full.reshape(-1, full.shape[-1])
-        middle = split + HEAD_K
-        wide = w_out.shape[1]
-        first_rows = full[:, :middle]
-        value_rows = full[:, middle + wide :]
-        full_out = full[:, middle : middle + wide]
+        )[None]
     else:
         full_conv = gather_conv(conv_weight)
         projections = gather_rows(jnp.concatenate([w_query, w_key, w_value], axis=1))

time: 144 us -> 131 us (0.910)
  Pallas kernels: 114 us -> 124 us
  matrix products: 9.81 us -> 0 us
  blocking collectives: 9.76 us -> 0 us
  local copies, waits for them, and re-layouts: 4.73 us -> 2.38 us
    pallas_call x1, Pallas kernels: 114 us -> 124 us  [encoder_stage(): pl.pallas_call(encoder_kernel, out_shape=jax.ShapeDtypeStruct((count, col...]
    dot_general x5 -> x0, matrix products: 9.81 us -> none  [the longest x1 3.9 us: body(): out = jnp.dot(mixed, full_out, preferred_element_type=jnp.float32)]
    all_gather x1 -> x0, blocking collectives: 9.76 us -> none  [body(): pair = lax.all_gather(pair, 'seq', axis=0, tiled=True)]
    broadcast_in_dim x3 -> x1, local copies, waits for them, and re-layouts: 3.83 us -> 0.61 us  [encoder_stage(): vectors[None]]
    concatenate x1 -> x2, other arithmetic: 0.01 us -> 1.5 us  [the longest x1 0.75 us: body(): jnp.concatenate([stem_bias, conv_gain, conv_bias, attn_gain])]
where the time goes in v4:
time: 131 us
  Pallas kernels  124 us (95%)
  other arithmetic  4.15 us (3%)
  local copies, waits for them, and re-layouts  2.38 us (2%)
    pallas_call x1, Pallas kernels, encoder_stage(): pl.pallas_call(encoder_kernel, out_shape=jax.ShapeDtypeStruct((count, col...  124 us

profile of v4, /device:TPU:8, one launch (start us, length us, event | category | flops | bytes accessed | tf_op | source)
XLA Modules:
  0.0 130.7 jit_solution(17046949813936896857)
XLA Ops:
  0.0 0.7 pad_maximum_fusion.3
  0.8 0.6 broadcast_in_dim.8.vector_ref
  1.4 0.3 fusion
  1.7 0.7 pad_maximum_fusion.1
  2.4 2.3 %pad_maximum_fusion = bf16[192,2880]{1,0:T(8,128)(2,1)} fusion(bf16[192,192]{1,0:T(8,128)(2,1)} %param.20, bf16[192,1536]{1,0:T(8,128)(2,1)} %param.21, bf16[192,128]{1,0:T(8,128)(2,1)} %param.19, bf16[192,1024]{1,0:T(8,128)(2,1)} %param.18), kind=kLoop, calls=%fused_computation | loop fusion | flops 4423680 | bytes 2211840 | tf_op jit(solution)/shard_map/concatenate | solution.py:664
  4.8 124.2 %encoder_stage.1 = bf16[128,1536]{1,0:T(8,128)(2,1)} custom-call(s32[128,128]{1,0:T(8,128)} %bitcast.5, bf16[60,768]{1,0:T(8,128)(2,1)} %stem_weight_ref.1, f32[1,4608]{1,0:T(1,128)} %broadcast_in_dim.8.vector_ref, f32[128,128]{1,0:T(8,128)} %get-tuple-element.8.cosine_ref, f32[128,128]{1,0:T(8,128)} %get-tuple-element.9.sine_ref, ...), custom_call_target="tpu_custom_call" | custom-call | tf_op jit(solution)/shard_map/encoder_stage/pallas_call | solution.py:578
  129.0 1.8 %copy.13 = bf16[1,128,1536]{2,1,0:T(8,128)(2,1)} copy(bf16[1,128,1536]{2,1,0:T(8,128)(2,1)} %bitcast.4) | data formatting | bytes 786432
  (2 shorter events, 0.0 us)

commit v5 on v4

--- a/solution.py
+++ b/solution.py
@@ -446,7 +446,7 @@
 
     width = 256
     steps = columns // width
-    group = 4
+    group = 8
     channels = ext_ref.shape[1]
     big = jnp.full((count, width), jnp.finfo(jnp.float32).max, jnp.float32)
 

time: 131 us -> 130 us (level)
  no operation moved by 1% of the time
where the time goes in v5:
time: 130 us
  Pallas kernels  124 us (95%)
  other arithmetic  4.15 us (3%)
  local copies, waits for them, and re-layouts  2.38 us (2%)
    pallas_call x1, Pallas kernels, encoder_stage(): pl.pallas_call(encoder_kernel, out_shape=jax.ShapeDtypeStruct((count, col...  124 us

profile of v5, /device:TPU:8, one launch (start us, length us, event | category | flops | bytes accessed | tf_op | source)
XLA Modules:
  0.0 130.1 jit_solution(8259345763683312693)
XLA Ops:
  0.0 0.7 pad_maximum_fusion.3
  0.8 0.6 broadcast_in_dim.8.vector_ref
  1.4 0.3 fusion
  1.7 0.7 pad_maximum_fusion.1
  2.4 2.3 %pad_maximum_fusion = bf16[192,2880]{1,0:T(8,128)(2,1)} fusion(bf16[192,192]{1,0:T(8,128)(2,1)} %param.20, bf16[192,1536]{1,0:T(8,128)(2,1)} %param.21, bf16[192,128]{1,0:T(8,128)(2,1)} %param.19, bf16[192,1024]{1,0:T(8,128)(2,1)} %param.18), kind=kLoop, calls=%fused_computation | loop fusion | flops 4423680 | bytes 2211840 | tf_op jit(solution)/shard_map/concatenate | solution.py:664
  4.8 123.6 %encoder_stage.1 = bf16[128,1536]{1,0:T(8,128)(2,1)} custom-call(s32[128,128]{1,0:T(8,128)} %bitcast.5, bf16[60,768]{1,0:T(8,128)(2,1)} %stem_weight_ref.1, f32[1,4608]{1,0:T(1,128)} %broadcast_in_dim.8.vector_ref, f32[128,128]{1,0:T(8,128)} %get-tuple-element.8.cosine_ref, f32[128,128]{1,0:T(8,128)} %get-tuple-element.9.sine_ref, ...), custom_call_target="tpu_custom_call" | custom-call | tf_op jit(solution)/shard_map/encoder_stage/pallas_call | solution.py:578
  128.4 1.8 %copy.13 = bf16[1,128,1536]{2,1,0:T(8,128)(2,1)} copy(bf16[1,128,1536]{2,1,0:T(8,128)(2,1)} %bitcast.4) | data formatting | bytes 786432
  (2 shorter events, 0.0 us)
